TPU v7x, 32 devices: a whole 2x2x4 slice. The times are simulated.
32 devices in a mesh: group: 2 (over y), clip: 4 (over x, core), seq: 4 (over z).
Axes of the slice: x: 2, y: 2, z: 4, core: 2. Of those that a mesh axis runs over, the one named last changes fastest.
Arguments:
- queries: bfloat16 [8, 512, 2048], P(('group', 'clip'), 'seq'), parts along dimension 0, may hold values from -18 to 18
- key_states: bfloat16 [8, 512, 2048], P(('group', 'clip'), 'seq'), parts along dimension 0, may hold values from -18 to 18
- value_states: bfloat16 [8, 512, 2048], P(('group', 'clip'), 'seq'), parts along dimension 0, may hold values from -6 to 6
- query_tangent: bfloat16 [8, 512, 2048], P(('group', 'clip'), 'seq'), parts along dimension 0, may hold values from -6 to 6
- key_tangent: bfloat16 [8, 512, 2048], P(('group', 'clip'), 'seq'), parts along dimension 0, may hold values from -6 to 6
- value_tangent: bfloat16 [8, 512, 2048], P(('group', 'clip'), 'seq'), parts along dimension 0, may hold values from -6 to 6
- offsets: int32 [8], P(('group', 'clip')), parts along dimension 0, may hold values from 0 to 130560
Outputs:
- attended: bfloat16 [8, 512, 2048], P(('group', 'clip'), 'seq'), parts along dimension 0
- attended_tangent: bfloat16 [8, 512, 2048], P(('group', 'clip'), 'seq'), parts along dimension 0
There are 2 independent parts, one for each index of `group`. A program takes and returns all parts, laid end to end along the dimension named above; each array names one. Nothing has to cross between parts.
All inputs are finite; a program needn't handle non-finite values.
Results may differ from a plain program's by a relative error of at most 0.012.
The roundings to bfloat16 on the way count: a program that leaves them out, or rounds other values in their place, can miss the bound.
Values may be sent and summed in bfloat16 or wider, within the bound.
No kernel may reach another device: no remote copies, remote signals or barrier semaphores. Data moves between devices by JAX's collectives and lax.ppermute only.
A program may use at most 64 MiB of HBM per device.

v0:
```python
import math
import jax
import jax.numpy as jnp
from jax import lax
from jax.sharding import PartitionSpec as P

H = 16
HD = 128
HH = 44
WW = 80
rope_theta = 10000.0


def rope_tables(first, count):
    global_index = first + jnp.arange(count, dtype=jnp.int32)
    frames = global_index // (HH * WW)
    grid_row = global_index // WW % HH
    column = global_index % WW
    spatial = HD // 6 * 2
    temporal = HD - 2 * spatial
    channel = jnp.arange(HD, dtype=jnp.int32)
    part_start = jnp.where(
        channel < temporal, 0, jnp.where(channel < temporal + spatial, temporal, temporal + spatial)
    )
    extent = jnp.where(channel < temporal, temporal, spatial)
    pair_index = (channel - part_start) // 2
    frequency = jnp.exp(
        -(2.0 * pair_index.astype(jnp.float32) / extent.astype(jnp.float32)) * math.log(rope_theta)
    )
    position = jnp.where(
        channel[None, :] < temporal,
        frames[:, None],
        jnp.where(channel[None, :] < temporal + spatial, grid_row[:, None], column[:, None]),
    )
    angles = position.astype(jnp.float32) * frequency[None, :]
    return (jnp.cos(angles)[:, None, :], jnp.sin(angles)[:, None, :])


def rotate(tensor, cosine, sine):
    channel = jnp.arange(tensor.shape[-1], dtype=jnp.int32)
    partner = jnp.where(
        channel % 2 == 0, -jnp.roll(tensor, -1, axis=-1), jnp.roll(tensor, 1, axis=-1)
    )
    return (tensor * cosine + partner * sine).astype(jnp.bfloat16)


def primal_terms(query_blk, keys_all, values_all, scaling):
    scores = (
        jnp.einsum("bhd,khd->hbk", query_blk, keys_all, preferred_element_type=jnp.float32)
        * scaling
    )
    largest = jnp.max(scores, axis=-1, keepdims=True)
    expons = jnp.exp(scores - largest)
    probs = expons / jnp.sum(expons, axis=-1, keepdims=True)
    weights = probs.astype(jnp.bfloat16)
    out_full = jnp.einsum("hbk,khd->bhd", weights, values_all, preferred_element_type=jnp.float32)
    return (weights, out_full)


def tangent_terms(
    query_blk, qdot_blk, keys_all, kdots_all, values_all, vdots_all, weights, out_full, scaling
):
    scores_dot = (
        jnp.einsum("bhd,khd->hbk", qdot_blk, keys_all, preferred_element_type=jnp.float32)
        + jnp.einsum("bhd,khd->hbk", query_blk, kdots_all, preferred_element_type=jnp.float32)
    ) * scaling
    product = weights.astype(jnp.float32) * scores_dot
    correction = jnp.sum(product, axis=-1)
    product_half = product.astype(jnp.bfloat16)
    tangent = (
        jnp.einsum("hbk,khd->bhd", weights, vdots_all, preferred_element_type=jnp.float32)
        + jnp.einsum("hbk,khd->bhd", product_half, values_all, preferred_element_type=jnp.float32)
        - jnp.transpose(correction)[:, :, None] * out_full
    )
    return tangent.astype(jnp.bfloat16)


def body(queries, key_states, value_states, query_tangent, key_tangent, value_tangent, offsets):
    devices = lax.axis_size("seq")
    repeat = max(devices // H, 1)
    per_device = max(H // devices, 1)
    groups = H // per_device
    width = per_device * HD
    tokens = queries.shape[1]
    sub_rows = tokens // repeat
    scaling = 1.0 / math.sqrt(HD)
    first = offsets[0] + lax.axis_index("seq") * tokens
    cosine, sine = rope_tables(first, tokens)

    def roped(array):
        return rotate(array[0].reshape(tokens, H, HD).astype(jnp.float32), cosine, sine).reshape(
            tokens, H * HD
        )

    def by_rows(array):
        shaped = array.reshape(repeat, sub_rows, groups, width)
        return jnp.transpose(shaped, (2, 0, 1, 3)).reshape(devices, sub_rows, width)

    def by_copies(array):
        shaped = jnp.transpose(array.reshape(tokens, groups, width), (1, 0, 2))
        spread = jnp.broadcast_to(shaped[:, None], (groups, repeat, tokens, width))
        return spread.reshape(devices, tokens, width)

    query_send = by_rows(roped(queries))
    qdot_send = by_rows(roped(query_tangent))
    key_send = by_copies(roped(key_states))
    kdot_send = by_copies(roped(key_tangent))
    value_send = by_copies(value_states[0])
    vdot_send = by_copies(value_tangent[0])
    query_rows = devices * sub_rows
    block = min(512, query_rows)
    count = query_rows // block

    def heads_view(array):
        return array.reshape(array.shape[0], per_device, HD)

    def blocks(array):
        return array.reshape(count, block, per_device, HD)

    received = (
        lax.all_to_all(query_send, "seq", split_axis=0, concat_axis=1, tiled=True),
        lax.all_to_all(key_send, "seq", split_axis=0, concat_axis=1, tiled=True),
        lax.all_to_all(value_send, "seq", split_axis=0, concat_axis=1, tiled=True),
        lax.all_to_all(qdot_send, "seq", split_axis=0, concat_axis=1, tiled=True),
        lax.all_to_all(kdot_send, "seq", split_axis=0, concat_axis=1, tiled=True),
        lax.all_to_all(vdot_send, "seq", split_axis=0, concat_axis=1, tiled=True),
    )
    query_in, key_in, value_in, qdot_in, kdot_in, vdot_in = tuple((array[0] for array in received))
    keys_all, values_all = (heads_view(key_in), heads_view(value_in))
    kdots_all, vdots_all = (heads_view(kdot_in), heads_view(vdot_in))

    def one_block(parts):
        query_blk, qdot_blk = parts
        weights, out_full = primal_terms(query_blk, keys_all, values_all, scaling)
        tangent = tangent_terms(
            query_blk,
            qdot_blk,
            keys_all,
            kdots_all,
            values_all,
            vdots_all,
            weights,
            out_full,
            scaling,
        )
        return (out_full.astype(jnp.bfloat16), tangent)

    attended, tangent_out = lax.map(one_block, (blocks(query_in), blocks(qdot_in)))

    def to_sources(array):
        return array.reshape(devices, sub_rows, width)

    returned = (
        lax.all_to_all(to_sources(attended), "seq", split_axis=0, concat_axis=0, tiled=True),
        lax.all_to_all(to_sources(tangent_out), "seq", split_axis=0, concat_axis=0, tiled=True),
    )

    def to_tokens(array):
        shaped = array.reshape(groups, repeat, sub_rows, width)
        return jnp.transpose(shaped, (1, 2, 0, 3)).reshape(tokens, H * HD)[None]

    return (to_tokens(returned[0]), to_tokens(returned[1]))


def solution(mesh):
    in_specs = (
        P(("group", "clip"), "seq", None),
        P(("group", "clip"), "seq", None),
        P(("group", "clip"), "seq", None),
        P(("group", "clip"), "seq", None),
        P(("group", "clip"), "seq", None),
        P(("group", "clip"), "seq", None),
        P(("group", "clip")),
    )
    out_specs = (P(("group", "clip"), "seq", None), P(("group", "clip"), "seq", None))
    return jax.shard_map(body, mesh=mesh, in_specs=in_specs, out_specs=out_specs, check_vma=False)
```

profile of v0, /device:TPU:0, one launch (start us, length us, event | category | flops | bytes accessed | tf_op | source)
XLA Modules:
  0.0 167.7 jit_solution(8478201329883006545)
XLA Ops:
  0.6 1.3 copy.48
  1.9 1.5 fusion.48
  3.7 1.2 fusion.50
  5.7 1.9 %maximum_negate_fusion.2 = (f32[128,16,128]{0,2,1:T(8,128)S(1)}, f32[128,16,128]{0,2,1:T(8,128)S(1)}) fusion(f32[128,16,1]{0,2,1:T(1,128)S(1)} %get-tuple-element.40, f32[128,16,127]{0,2,1:T(8,128)} %get-tuple-element.42, f32[128,16,127]{0,2,1:T(8,128)} %get-tuple-element.41, f32[128,16,1]{0,2,1:T(1,128)S(1)} %get-tuple-element.39), kind=kLoop, calls=%fused_computation.26 | loop fusion | flops 786432 | bytes 4194304 | tf_op jit(solution)/shard_map/neg | solution.py:42
  8.4 1.8 %fusion.24 = (bf16[4,128,512]{1,2,0:T(8,128)(2,1)}, bf16[4,128,512]{1,2,0:T(8,128)(2,1)}) fusion(f32[1,128,4,512]{1,3,2,0:T(8,128)S(1)} %bitcast.120, f32[1,128,4,512]{1,3,2,0:T(8,128)S(1)} %bitcast.122, f32[1,128,4,512]{1,3,2,0:T(8,128)S(1)} %bitcast.123, f32[1,128,4,512]{1,3,2,0:T(8,128)S(1)} %bitcast.108, f32[1,128,4,512]{1,3,2,0:T(8,128)S(1)} %bitcast.118, ...), kind=kLoop, calls=%fused_computation.35 | loop fusion | flops 2621440 | bytes 9437696 | tf_op jit(solution)/shard_map/reshape | solution.py:97
  10.1 6.3 %all-to-all-start = ((bf16[4,128,512]{1,2,0:T(8,128)(2,1)}), bf16[4,128,512]{1,2,0:T(8,128)(2,1)}, u32[]{:S(2)}, u32[]{:S(2)}) async-start(bf16[4,128,512]{1,2,0:T(8,128)(2,1)} %get-tuple-element.25), calls=%async_computation | async-start | bytes 1048576 | tf_op jit(solution)/shard_map/all_to_all | solution.py:121
  16.5 1.2 copy.35
  17.7 1.5 fusion.51
  19.2 1.2 copy.53
  20.7 1.0 copy-done.6
  22.6 0.6 copy-done.1
  23.2 1.7 %fusion.25 = (bf16[4,128,512]{1,2,0:T(8,128)(2,1)}, bf16[4,128,512]{1,2,0:T(8,128)(2,1)}) fusion(f32[128,4,512]{0,2,1:T(8,128)S(1)} %bitcast.117, pred[512]{0:T(512)(128)(4,1)S(1)} %broadcast_bitcast_fusion, f32[128,4,512]{0,2,1:T(8,128)S(1)} %bitcast.114, f32[128,4,512]{0,2,1:T(8,128)S(1)} %bitcast.121, f32[128,4,512]{0,2,1:T(8,128)S(1)} %bitcast.129, ...), kind=kLoop, calls=%fused_computation.36 | loop fusion | flops 2621440 | bytes 9437696 | tf_op jit(solution)/shard_map/transpose | solution.py:100
  25.0 6.1 %all-to-all-done = bf16[4,128,512]{1,2,0:T(8,128)(2,1)} async-done(((bf16[4,128,512]{1,2,0:T(8,128)(2,1)}), bf16[4,128,512]{1,2,0:T(8,128)(2,1)}, u32[]{:S(2)}, u32[]{:S(2)}) %all-to-all-start) | async-done | bytes 524320 | tf_op jit(solution)/shard_map/all_to_all | solution.py:121
  31.1 17.5 %all_to_all.64 = bf16[4,128,512]{1,2,0:T(8,128)(2,1)S(1)} all-to-all(bf16[4,128,512]{1,2,0:T(8,128)(2,1)} %get-tuple-element.23), channel_id=1, replica_groups=mesh['group'=2,'clip'=4,'seq'=4] {'seq'}, dimensions={0} | all-to-all | bytes 1048576 | tf_op jit(solution)/shard_map/all_to_all | solution.py:122
  48.6 17.7 %all_to_all.65 = bf16[4,128,512]{1,2,0:T(8,128)(2,1)} all-to-all(bf16[4,128,512]{1,2,0:T(8,128)(2,1)} %get-tuple-element.24), channel_id=1, replica_groups=mesh['group'=2,'clip'=4,'seq'=4] {'seq'}, dimensions={0} | all-to-all | bytes 1048576 | tf_op jit(solution)/shard_map/all_to_all | solution.py:124
  66.3 3.5 %all-to-all-start.6 = ((bf16[4,128,512]{1,2,0:T(8,128)(2,1)}), bf16[4,128,512]{1,2,0:T(8,128)(2,1)S(1)}, u32[]{:S(2)}, u32[]{:S(2)}) async-start(bf16[4,128,512]{1,2,0:T(8,128)(2,1)} %get-tuple-element.22), calls=%async_computation.6 | async-start | bytes 1048576 | tf_op jit(solution)/shard_map/all_to_all | solution.py:125
  69.7 1.4 reshape_squeeze.25
  71.2 0.9 copy.94
  72.4 0.9 copy.93
  73.3 1.2 copy.34
  75.1 8.2 %all-to-all-done.6 = bf16[4,128,512]{1,2,0:T(8,128)(2,1)S(1)} async-done(((bf16[4,128,512]{1,2,0:T(8,128)(2,1)}), bf16[4,128,512]{1,2,0:T(8,128)(2,1)S(1)}, u32[]{:S(2)}, u32[]{:S(2)}) %all-to-all-start.6) | async-done | bytes 524320 | tf_op jit(solution)/shard_map/all_to_all | solution.py:125
  83.3 3.5 %all-to-all-start.2 = ((bf16[4,128,512]{2,1,0:T(8,128)(2,1)}), bf16[4,128,512]{2,1,0:T(8,128)(2,1)S(1)}, u32[]{:S(2)}, u32[]{:S(2)}) async-start(bf16[4,128,512]{2,1,0:T(8,128)(2,1)} %bitcast.100), calls=%async_computation.2 | async-start | bytes 1048576 | tf_op jit(solution)/shard_map/all_to_all | solution.py:123
  86.8 0.7 fusion.35
  87.5 3.1 %fusion.53 = (f32[4,512]{1,0:T(4,128)S(1)}, f32[4,512,512]{1,2,0:T(8,128)}) fusion(f32[4,512,512]{1,2,0:T(8,128)S(1)} %fusion.35), kind=kOutput, calls=%fused_computation.82 | output fusion | flops 4194815 | bytes 8396800 | tf_op jit(solution)/shard_map/while/body/eval_jaxpr/sub | solution.py:53
  90.6 10.2 %all-to-all-done.2 = bf16[4,128,512]{2,1,0:T(8,128)(2,1)S(1)} async-done(((bf16[4,128,512]{2,1,0:T(8,128)(2,1)}), bf16[4,128,512]{2,1,0:T(8,128)(2,1)S(1)}, u32[]{:S(2)}, u32[]{:S(2)}) %all-to-all-start.2) | async-done | bytes 524320 | tf_op jit(solution)/shard_map/all_to_all | solution.py:123
  100.8 4.3 %all-to-all-start.4 = ((bf16[4,128,512]{2,1,0:T(8,128)(2,1)}), bf16[4,128,512]{2,1,0:T(8,128)(2,1)}, u32[]{:S(2)}, u32[]{:S(2)}) async-start(bf16[4,128,512]{2,1,0:T(8,128)(2,1)} %bitcast.99), calls=%async_computation.4 | async-start | bytes 1048576 | tf_op jit(solution)/shard_map/all_to_all | solution.py:126
  105.1 2.8 %divide_convert_fusion = bf16[4,512,512]{1,2,0:T(8,128)(2,1)S(1)} fusion(f32[4,512,512]{1,2,0:T(8,128)} %get-tuple-element.54, f32[4,512]{1,0:T(4,128)S(1)} %get-tuple-element.53), kind=kLoop, calls=%fused_computation.2 | loop fusion | flops 2097152 | bytes 6299648 | tf_op jit(solution)/shard_map/while/body/eval_jaxpr/convert_element_type | solution.py:55
  107.9 2.0 %copy.50 = bf16[4,128,512]{2,1,0:T(8,128)(2,1)} copy(bf16[4,128,512]{1,2,0:T(8,128)(2,1)} %all_to_all.65) | data formatting | bytes 1048576 | tf_op jit(solution)/shard_map/all_to_all | solution.py:124
  109.9 2.0 %squeeze.14 = bf16[512,4,128]{2,1,0:T(4,128)(2,1)} reshape(bf16[4,128,512]{2,1,0:T(8,128)(2,1)} %copy.50) | data formatting | bytes 1048576 | tf_op jit(solution)/shard_map/while/body/jit(dynamic_index_in_dim)/squeeze | solution.py:148
  111.9 1.0 copy.55
  112.9 1.9 %reshape_squeeze.29 = bf16[512,4,128]{2,1,0:T(4,128)(2,1)} reshape(bf16[4,128,512]{2,1,0:T(8,128)(2,1)} %copy.55) | data formatting | bytes 1048576 | tf_op jit(solution)/shard_map/reshape;squeeze | solution.py:115
  114.9 1.2 reshape_squeeze.26
  116.0 2.0 %fusion.54 = (bf16[512,4,128]{2,0,1:T(8,128)(2,1)}, f32[512,4,128]{2,0,1:T(8,128)}) fusion(bf16[4,512,512]{1,2,0:T(8,128)(2,1)S(1)} %divide_convert_fusion, bf16[512,4,128]{2,1,0:T(4,128)(2,1)S(1)} %reshape_squeeze.26), kind=kOutput, calls=%fused_computation.83 | convolution fusion | flops 268697600 | bytes 4194304 | tf_op jit(solution)/shard_map/while/body/eval_jaxpr/hbk,khd->bhd/dot_general | solution.py:56
  118.1 2.7 %fusion.28 = f32[4,512,512]{1,2,0:T(8,128)} fusion(bf16[512,4,128]{2,1,0:T(4,128)(2,1)S(1)} %copy-done.8, bf16[512,4,128]{2,1,0:T(4,128)(2,1)S(1)} %reshape_squeeze.24), kind=kOutput, calls=%fused_computation.39 | convolution fusion | flops 268435456 | bytes 5242880 | tf_op jit(solution)/shard_map/while/body/eval_jaxpr/bhd,khd->hbk/dot_general | solution.py:64
  120.8 2.0 %reshape_squeeze.28 = bf16[512,4,128]{2,1,0:T(4,128)(2,1)} reshape(bf16[4,128,512]{2,1,0:T(8,128)(2,1)} %all-to-all-done.4) | data formatting | bytes 1048576 | tf_op jit(solution)/shard_map/reshape;squeeze | solution.py:115
  122.8 1.9 %fusion.30 = f32[4,512,128]{2,1,0:T(8,128)S(1)} fusion(bf16[4,512,512]{1,2,0:T(8,128)(2,1)S(1)} %divide_convert_fusion, bf16[512,4,128]{2,1,0:T(4,128)(2,1)} %reshape_squeeze.28), kind=kOutput, calls=%fused_computation.41 | convolution fusion | flops 268435456 | bytes 3670016 | tf_op jit(solution)/shard_map/while/body/eval_jaxpr/hbk,khd->bhd/dot_general | solution.py:71
  124.7 3.5 %fusion.55 = (f32[4,512]{1,0:T(4,128)S(1)}, bf16[4,512,512]{1,2,0:T(8,128)(2,1)S(1)}) fusion(f32[4,512,512]{1,2,0:T(8,128)} %fusion.28, bf16[512,4,128]{2,1,0:T(4,128)(2,1)} %reshape_squeeze.29, bf16[512,4,128]{2,1,0:T(4,128)(2,1)S(1)} %copy-done.3, bf16[4,512,512]{1,2,0:T(8,128)(2,1)S(1)} %divide_convert_fusion), kind=kOutput, calls=%fused_computation.84 | convolution fusion | flops 274724864 | bytes 9445376 | tf_op jit(solution)/shard_map/while/body/eval_jaxpr/bhd,khd->hbk/dot_general | solution.py:65
  128.2 0.9 fusion.16
  129.1 0.4 copy.60
  129.5 1.0 reshape.425
  130.5 4.9 %all-to-all-start.7 = ((bf16[4,128,512]{2,1,0:T(8,128)(2,1)}), bf16[4,128,512]{2,1,0:T(8,128)(2,1)S(1)}, u32[]{:S(2)}, u32[]{:S(2)}) async-start(bf16[4,128,512]{2,1,0:T(8,128)(2,1)} %reshape.425), calls=%async_computation.7 | async-start | bytes 1048576 | tf_op jit(solution)/shard_map/all_to_all | solution.py:155
  135.4 0.4 copy.43
  135.8 1.0 reshape.422
  136.8 12.1 %all-to-all-done.7 = bf16[4,128,512]{2,1,0:T(8,128)(2,1)S(1)} async-done(((bf16[4,128,512]{2,1,0:T(8,128)(2,1)}), bf16[4,128,512]{2,1,0:T(8,128)(2,1)S(1)}, u32[]{:S(2)}, u32[]{:S(2)}) %all-to-all-start.7) | async-done | bytes 524320 | tf_op jit(solution)/shard_map/all_to_all | solution.py:155
  148.9 3.5 %all-to-all-start.3 = ((bf16[4,128,512]{2,1,0:T(8,128)(2,1)}), bf16[4,128,512]{2,1,0:T(8,128)(2,1)S(1)}, u32[]{:S(2)}, u32[]{:S(2)}) async-start(bf16[4,128,512]{2,1,0:T(8,128)(2,1)} %reshape.422), calls=%async_computation.3 | async-start | bytes 1048576 | tf_op jit(solution)/shard_map/all_to_all | solution.py:154
  152.6 1.0 copy.63
  153.7 12.7 %all-to-all-done.3 = bf16[4,128,512]{2,1,0:T(8,128)(2,1)S(1)} async-done(((bf16[4,128,512]{2,1,0:T(8,128)(2,1)}), bf16[4,128,512]{2,1,0:T(8,128)(2,1)S(1)}, u32[]{:S(2)}, u32[]{:S(2)}) %all-to-all-start.3) | async-done | bytes 524320 | tf_op jit(solution)/shard_map/all_to_all | solution.py:154
  166.6 1.0 copy.62
  (49 shorter events, 3.6 us)
Async XLA Ops:
  0.6 2.8 %copy-start.11 = (bf16[1,128,2048]{2,1,0:T(8,128)(2,1)S(1)}, bf16[1,128,2048]{2,1,0:T(8,128)(2,1)}, u32[]{:S(2)}) copy-start(bf16[1,128,2048]{2,1,0:T(8,128)(2,1)} %param.7) | copy-start | bytes 1572868
  5.6 2.0 %copy-start.5 = (f32[128,16,127]{0,2,1:T(8,128)S(1)}, f32[128,16,127]{0,2,1:T(8,128)}, u32[]{:S(2)}) copy-start(f32[128,16,127]{0,2,1:T(8,128)} %get-tuple-element.46) | copy-start | bytes 3121156
  8.4 1.8 %copy-start = (f32[128,16,128]{0,2,1:T(8,128)}, f32[128,16,128]{0,2,1:T(8,128)S(1)}, u32[]{:S(2)}) copy-start(f32[128,16,128]{0,2,1:T(8,128)S(1)} %mul.164) | copy-start | bytes 3145732
  10.1 20.9 %all-to-all-start = ((bf16[4,128,512]{1,2,0:T(8,128)(2,1)}), bf16[4,128,512]{1,2,0:T(8,128)(2,1)}, u32[]{:S(2)}, u32[]{:S(2)}) async-start(bf16[4,128,512]{1,2,0:T(8,128)(2,1)} %get-tuple-element.25), calls=%async_computation | async-start | bytes 1048576 | tf_op jit(solution)/shard_map/all_to_all | solution.py:121
  20.4 1.2 copy-start.6
  20.5 1.5 copy-start.7
  22.0 1.2 copy-start.1
  25.0 47.1 %copy-start.12 = (bf16[1,128,2048]{2,1,0:T(8,128)(2,1)S(1)}, bf16[1,128,2048]{2,1,0:T(8,128)(2,1)}, u32[]{:S(2)}) copy-start(bf16[1,128,2048]{2,1,0:T(8,128)(2,1)} %param.12) | copy-start | bytes 1572868
  66.3 17.0 %all-to-all-start.6 = ((bf16[4,128,512]{1,2,0:T(8,128)(2,1)}), bf16[4,128,512]{1,2,0:T(8,128)(2,1)S(1)}, u32[]{:S(2)}, u32[]{:S(2)}) async-start(bf16[4,128,512]{1,2,0:T(8,128)(2,1)} %get-tuple-element.22), calls=%async_computation.6 | async-start | bytes 1048576 | tf_op jit(solution)/shard_map/all_to_all | solution.py:125
  74.7 12.8 %copy-start.2 = (bf16[512,4,128]{2,1,0:T(4,128)(2,1)}, bf16[512,4,128]{2,1,0:T(4,128)(2,1)S(1)}, u32[]{:S(2)}) copy-start(bf16[512,4,128]{2,1,0:T(4,128)(2,1)S(1)} %squeeze.13) | copy-start | bytes 1572868
  83.3 17.5 %all-to-all-start.2 = ((bf16[4,128,512]{2,1,0:T(8,128)(2,1)}), bf16[4,128,512]{2,1,0:T(8,128)(2,1)S(1)}, u32[]{:S(2)}, u32[]{:S(2)}) async-start(bf16[4,128,512]{2,1,0:T(8,128)(2,1)} %bitcast.100), calls=%async_computation.2 | async-start | bytes 1048576 | tf_op jit(solution)/shard_map/all_to_all | solution.py:123
  100.8 4.3 %copy-start.9 = (bf16[4,128,512]{2,1,0:T(8,128)(2,1)}, bf16[4,128,512]{2,1,0:T(8,128)(2,1)S(1)}, u32[]{:S(2)}) copy-start(bf16[4,128,512]{2,1,0:T(8,128)(2,1)S(1)} %all-to-all-done.2) | copy-start | bytes 1572868
  100.8 20.0 %all-to-all-start.4 = ((bf16[4,128,512]{2,1,0:T(8,128)(2,1)}), bf16[4,128,512]{2,1,0:T(8,128)(2,1)}, u32[]{:S(2)}, u32[]{:S(2)}) async-start(bf16[4,128,512]{2,1,0:T(8,128)(2,1)} %bitcast.99), calls=%async_computation.4 | async-start | bytes 1048576 | tf_op jit(solution)/shard_map/all_to_all | solution.py:126
  116.0 2.1 %copy-start.8 = (bf16[512,4,128]{2,1,0:T(4,128)(2,1)S(1)}, bf16[512,4,128]{2,1,0:T(4,128)(2,1)}, u32[]{:S(2)}) copy-start(bf16[512,4,128]{2,1,0:T(4,128)(2,1)} %squeeze.14) | copy-start | bytes 1572868
  120.7 4.0 %copy-start.3 = (bf16[512,4,128]{2,1,0:T(4,128)(2,1)S(1)}, bf16[512,4,128]{2,1,0:T(4,128)(2,1)}, u32[]{:S(2)}) copy-start(bf16[512,4,128]{2,1,0:T(4,128)(2,1)} %copy-done.2) | copy-start | bytes 1572868
  124.7 3.5 %copy-start.4 = (f32[512,4,128]{2,0,1:T(8,128)S(1)}, f32[512,4,128]{2,0,1:T(8,128)}, u32[]{:S(2)}) copy-start(f32[512,4,128]{2,0,1:T(8,128)} %get-tuple-element.56) | copy-start | bytes 3145732
  128.2 7.2 %copy-start.10 = (bf16[512,4,128]{2,0,1:T(8,128)(2,1)S(1)}, bf16[512,4,128]{2,0,1:T(8,128)(2,1)}, u32[]{:S(2)}) copy-start(bf16[512,4,128]{2,0,1:T(8,128)(2,1)} %get-tuple-element.55) | copy-start | bytes 1572868
  130.5 18.4 %all-to-all-start.7 = ((bf16[4,128,512]{2,1,0:T(8,128)(2,1)}), bf16[4,128,512]{2,1,0:T(8,128)(2,1)S(1)}, u32[]{:S(2)}, u32[]{:S(2)}) async-start(bf16[4,128,512]{2,1,0:T(8,128)(2,1)} %reshape.425), calls=%async_computation.7 | async-start | bytes 1048576 | tf_op jit(solution)/shard_map/all_to_all | solution.py:155
  148.9 17.5 %all-to-all-start.3 = ((bf16[4,128,512]{2,1,0:T(8,128)(2,1)}), bf16[4,128,512]{2,1,0:T(8,128)(2,1)S(1)}, u32[]{:S(2)}, u32[]{:S(2)}) async-start(bf16[4,128,512]{2,1,0:T(8,128)(2,1)} %reshape.422), calls=%async_computation.3 | async-start | bytes 1048576 | tf_op jit(solution)/shard_map/all_to_all | solution.py:154
where the time goes:
time: 169 us; the launch traced here: 168 us
  waiting for transfers between devices  49.3 us (29%)
  blocking collectives  35.2 us (21%)
  local copies, waits for them, and re-layouts  31.4 us (19%)
  starting transfers between devices  25.9 us (15%)
  other arithmetic  12.5 us (7%)
  matrix products  11.7 us (7%)
    all_to_all x1, blocking collectives, body(): lax.all_to_all(qdot_send, 'seq', split_axis=0, concat_axis=1, tiled=True)  17.7 us
    all_to_all x1, blocking collectives, body(): lax.all_to_all(key_send, 'seq', split_axis=0, concat_axis=1, tiled=True)  17.5 us
    all_to_all x1, waiting for transfers between devices, body(): lax.all_to_all(to_sources(attended), 'seq', split_axis=0, concat_axis=0,...  12.7 us
    all_to_all x1, waiting for transfers between devices, body(): lax.all_to_all(to_sources(tangent_out), 'seq', split_axis=0, concat_axis=...  12.1 us
    all_to_all x1, waiting for transfers between devices, body(): lax.all_to_all(value_send, 'seq', split_axis=0, concat_axis=1, tiled=True)  10.2 us
    all_to_all x1, waiting for transfers between devices, body(): lax.all_to_all(kdot_send, 'seq', split_axis=0, concat_axis=1, tiled=True)  8.22 us
    all_to_all x1, starting transfers between devices, body(): lax.all_to_all(query_send, 'seq', split_axis=0, concat_axis=1, tiled=True)  6.35 us
    all_to_all x1, waiting for transfers between devices, body(): lax.all_to_all(query_send, 'seq', split_axis=0, concat_axis=1, tiled=True)  6.11 us
  transfers between devices with their start and end apart: 6, of which 5 were waited for; matrix products, arithmetic and copies ran while one was open for 20% of the time, Pallas kernels for 0%

commit v1 on v0

--- a/solution.py
+++ b/solution.py
@@ -9,6 +9,22 @@
 HH = 44
 WW = 80
 rope_theta = 10000.0
+
+
+def swapped_with_each(shard, axis, split, join):
+    ways, here = (lax.axis_size(axis), lax.axis_index(axis))
+    width = shard.shape[split] // ways
+    shape = list(shard.shape)
+    shape[split] = width
+    height = shape[join]
+    shape[join] = height * ways
+    full = jnp.zeros(shape, shard.dtype)
+    for mask in range(ways):
+        part = lax.dynamic_slice_in_dim(shard, (here ^ mask) * width, width, axis=split)
+        if mask:
+            part = lax.ppermute(part, axis, [(d, d ^ mask) for d in range(ways)])
+        full = lax.dynamic_update_slice_in_dim(full, part, (here ^ mask) * height, axis=join)
+    return full
 
 
 def rope_tables(first, count):
@@ -152,7 +168,7 @@
 
     returned = (
         lax.all_to_all(to_sources(attended), "seq", split_axis=0, concat_axis=0, tiled=True),
-        lax.all_to_all(to_sources(tangent_out), "seq", split_axis=0, concat_axis=0, tiled=True),
+        swapped_with_each(to_sources(tangent_out), "seq", 0, 0),
     )
 
     def to_tokens(array):

time: 169 us -> 159 us (0.941)
  blocking collectives: 35.2 us -> 0 us
  starting transfers between devices: 25.9 us -> 34.6 us
  local copies, waits for them, and re-layouts: 31.4 us -> 38.2 us
  matrix products: 11.7 us -> 15.9 us
  waiting for transfers between devices: 49.3 us -> 53.1 us
  other arithmetic: 12.5 us -> 14.5 us
    all_to_all x2 -> x0, blocking collectives: 35.2 us -> none  [the longest x1 17.7 us: body(): lax.all_to_all(qdot_send, 'seq', split_axis=0, concat_axis=1, tiled=True)]
    all_to_all x1, waiting for transfers between devices: 12.7 us -> 0.01 us  [body(): lax.all_to_all(to_sources(attended), 'seq', split_axis=0, concat_axis=0,...]
    all_to_all x1, waiting for transfers between devices: 0.01 us -> 9.55 us  [body(): lax.all_to_all(vdot_send, 'seq', split_axis=0, concat_axis=1, tiled=True)]
    ppermute x0 -> x3, waiting for transfers between devices: none -> 8.58 us  [swapped_with_each(): part = lax.ppermute(part, axis, [(d, d ^ mask) for d in range(ways)])]
    all_to_all x1, waiting for transfers between devices: 8.22 us -> 0.01 us  [body(): lax.all_to_all(kdot_send, 'seq', split_axis=0, concat_axis=1, tiled=True)]
    all_to_all x1 -> x2, starting transfers between devices: 4.86 us -> 10.5 us  [the longest x1 6.35 us: body(): lax.all_to_all(key_send, 'seq', split_axis=0, concat_axis=1, tiled=True)]
    all_to_all x1, waiting for transfers between devices: 6.11 us -> 11.7 us  [body(): lax.all_to_all(query_send, 'seq', split_axis=0, concat_axis=1, tiled=True)]
    dynamic_update_slice x0 -> x5, local copies, waits for them, and re-layouts: none -> 4.89 us  [swapped_with_each(): lax.dynamic_update_slice_in_dim(full, part, (here ^ mask) * height, axis=...]
  transfers between devices with their start and end apart: 6 -> 10, of which waited for: 5 -> 7; matrix products, arithmetic and copies ran while one was open for 20% -> 36% of each run, Pallas kernels for 0% -> 0%
where the time goes in v1:
time: 159 us; the launch traced here: 158 us
  waiting for transfers between devices  53.1 us (33%)
  local copies, waits for them, and re-layouts  38.2 us (24%)
  starting transfers between devices  34.6 us (22%)
  matrix products  15.9 us (10%)
  other arithmetic  14.5 us (9%)
  between operations  1.74 us (1%)
    all_to_all x1, waiting for transfers between devices, body(): lax.all_to_all(value_send, 'seq', split_axis=0, concat_axis=1, tiled=True)  12.7 us
    all_to_all x1, waiting for transfers between devices, body(): lax.all_to_all(query_send, 'seq', split_axis=0, concat_axis=1, tiled=True)  11.7 us
    all_to_all x1, waiting for transfers between devices, body(): lax.all_to_all(vdot_send, 'seq', split_axis=0, concat_axis=1, tiled=True)  9.55 us
    ppermute x3, waiting for transfers between devices, swapped_with_each(): part = lax.ppermute(part, axis, [(d, d ^ mask) for d in range(ways)])  8.58 us
    sub x1, other arithmetic, primal_terms(): expons = jnp.exp(scores - largest)  6.78 us
    all_to_all x1, starting transfers between devices, body(): lax.all_to_all(key_send, 'seq', split_axis=0, concat_axis=1, tiled=True)  6.35 us
    all_to_all x1, waiting for transfers between devices, body(): lax.all_to_all(key_send, 'seq', split_axis=0, concat_axis=1, tiled=True)  6.15 us
    convert_element_type x4, local copies, waits for them, and re-layouts, roped(): array[0].reshape(tokens, H, HD).astype(jnp.float32)  4.97 us
  transfers between devices with their start and end apart: 10, of which 7 were waited for; matrix products, arithmetic and copies ran while one was open for 36% of the time, Pallas kernels for 0%

profile of v1, /device:TPU:0, one launch (start us, length us, event | category | flops | bytes accessed | tf_op | source)
XLA Modules:
  0.0 158.0 jit_solution(2869267563646686244)
XLA Ops:
  1.4 1.2 copy.58
  2.6 1.1 fusion.45
  3.8 1.2 copy.40
  5.3 1.0 copy-done.5
  7.4 1.7 %fusion.25 = (bf16[4,128,512]{1,2,0:T(8,128)(2,1)}, bf16[4,128,512]{1,2,0:T(8,128)(2,1)}) fusion(f32[128,4,512]{0,2,1:T(8,128)S(1)} %bitcast.111, pred[512]{0:T(512)(128)(4,1)S(1)} %broadcast_bitcast_fusion, f32[128,4,512]{0,2,1:T(8,128)S(1)} %bitcast.114, f32[128,4,512]{0,2,1:T(8,128)S(1)} %bitcast.121, f32[128,4,512]{0,2,1:T(8,128)S(1)} %bitcast.126, ...), kind=kLoop, calls=%fused_computation.36 | loop fusion | flops 2621440 | bytes 9437696 | tf_op jit(solution)/shard_map/transpose | solution.py:116
  9.1 6.3 %all-to-all-start.1 = ((bf16[4,128,512]{1,2,0:T(8,128)(2,1)}), bf16[4,128,512]{1,2,0:T(8,128)(2,1)}, u32[]{:S(2)}, u32[]{:S(2)}) async-start(bf16[4,128,512]{1,2,0:T(8,128)(2,1)} %get-tuple-element.23), calls=%async_computation.1 | async-start | bytes 1048576 | tf_op jit(solution)/shard_map/all_to_all | solution.py:138
  15.4 1.2 copy.53
  16.7 1.5 fusion.48
  18.2 1.2 copy.37
  19.7 1.0 copy-done.6
  22.2 1.7 %fusion.24 = (bf16[4,128,512]{1,2,0:T(8,128)(2,1)}, bf16[4,128,512]{1,2,0:T(8,128)(2,1)}) fusion(f32[1,128,4,512]{1,3,2,0:T(8,128)S(1)} %bitcast.122, f32[1,128,4,512]{1,3,2,0:T(8,128)S(1)} %bitcast.129, f32[1,128,4,512]{1,3,2,0:T(8,128)S(1)} %bitcast.130, f32[1,128,4,512]{1,3,2,0:T(8,128)S(1)} %bitcast.117, f32[1,128,4,512]{1,3,2,0:T(8,128)S(1)} %bitcast.124, ...), kind=kLoop, calls=%fused_computation.35 | loop fusion | flops 2621440 | bytes 9437696 | tf_op jit(solution)/shard_map/reshape | solution.py:113
  23.9 6.1 %all-to-all-done.1 = bf16[4,128,512]{1,2,0:T(8,128)(2,1)} async-done(((bf16[4,128,512]{1,2,0:T(8,128)(2,1)}), bf16[4,128,512]{1,2,0:T(8,128)(2,1)}, u32[]{:S(2)}, u32[]{:S(2)}) %all-to-all-start.1) | async-done | bytes 524320 | tf_op jit(solution)/shard_map/all_to_all | solution.py:138
  30.0 3.5 %all-to-all-start = ((bf16[4,128,512]{1,2,0:T(8,128)(2,1)}), bf16[4,128,512]{1,2,0:T(8,128)(2,1)S(1)}, u32[]{:S(2)}, u32[]{:S(2)}) async-start(bf16[4,128,512]{1,2,0:T(8,128)(2,1)} %get-tuple-element.25), calls=%async_computation | async-start | bytes 1048576 | tf_op jit(solution)/shard_map/all_to_all | solution.py:137
  33.5 1.4 reshape_squeeze.25
  35.8 11.7 %all-to-all-done = bf16[4,128,512]{1,2,0:T(8,128)(2,1)S(1)} async-done(((bf16[4,128,512]{1,2,0:T(8,128)(2,1)}), bf16[4,128,512]{1,2,0:T(8,128)(2,1)S(1)}, u32[]{:S(2)}, u32[]{:S(2)}) %all-to-all-start) | async-done | bytes 524320 | tf_op jit(solution)/shard_map/all_to_all | solution.py:137
  47.5 3.5 %all-to-all-start.2 = ((bf16[4,128,512]{2,1,0:T(8,128)(2,1)}), bf16[4,128,512]{2,1,0:T(8,128)(2,1)S(1)}, u32[]{:S(2)}, u32[]{:S(2)}) async-start(bf16[4,128,512]{2,1,0:T(8,128)(2,1)} %bitcast.103), calls=%async_computation.2 | async-start | bytes 1048576 | tf_op jit(solution)/shard_map/all_to_all | solution.py:139
  51.4 0.9 copy.99
  52.3 12.7 %all-to-all-done.2 = bf16[4,128,512]{2,1,0:T(8,128)(2,1)S(1)} async-done(((bf16[4,128,512]{2,1,0:T(8,128)(2,1)}), bf16[4,128,512]{2,1,0:T(8,128)(2,1)S(1)}, u32[]{:S(2)}, u32[]{:S(2)}) %all-to-all-start.2) | async-done | bytes 524320 | tf_op jit(solution)/shard_map/all_to_all | solution.py:139
  65.0 3.5 %all-to-all-start.4 = ((bf16[4,128,512]{2,1,0:T(8,128)(2,1)}), bf16[4,128,512]{2,1,0:T(8,128)(2,1)S(1)}, u32[]{:S(2)}, u32[]{:S(2)}) async-start(bf16[4,128,512]{2,1,0:T(8,128)(2,1)} %bitcast.102), calls=%async_computation.4 | async-start | bytes 1048576 | tf_op jit(solution)/shard_map/all_to_all | solution.py:142
  68.5 1.2 copy.42
  70.3 2.7 %fusion.35 = f32[4,512,512]{1,2,0:T(8,128)} fusion(bf16[512,4,128]{2,1,0:T(4,128)(2,1)S(1)} %reshape_squeeze.24, bf16[512,4,128]{2,1,0:T(4,128)(2,1)S(1)} %squeeze.13), kind=kOutput, calls=%fused_computation.48 | convolution fusion | flops 268435456 | bytes 5242880 | tf_op jit(solution)/shard_map/while/body/eval_jaxpr/bhd,khd->hbk/dot_general | solution.py:65
  73.0 9.6 %all-to-all-done.4 = bf16[4,128,512]{2,1,0:T(8,128)(2,1)S(1)} async-done(((bf16[4,128,512]{2,1,0:T(8,128)(2,1)}), bf16[4,128,512]{2,1,0:T(8,128)(2,1)S(1)}, u32[]{:S(2)}, u32[]{:S(2)}) %all-to-all-start.4) | async-done | bytes 524320 | tf_op jit(solution)/shard_map/all_to_all | solution.py:142
  82.5 4.1 %all-to-all-start.5 = ((bf16[4,128,512]{1,2,0:T(8,128)(2,1)}), bf16[4,128,512]{1,2,0:T(8,128)(2,1)}, u32[]{:S(2)}, u32[]{:S(2)}) async-start(bf16[4,128,512]{1,2,0:T(8,128)(2,1)} %get-tuple-element.24), calls=%async_computation.5 | async-start | bytes 1048576 | tf_op jit(solution)/shard_map/all_to_all | solution.py:140
  86.7 6.8 %fusion.53 = (f32[4,512]{1,0:T(4,128)S(1)}, f32[4,512,512]{1,2,0:T(8,128)}) fusion(f32[4,512,512]{1,2,0:T(8,128)} %fusion.35), kind=kOutput, calls=%fused_computation.87 | output fusion | flops 4194815 | bytes 8396800 | tf_op jit(solution)/shard_map/while/body/eval_jaxpr/sub | solution.py:69
  93.6 2.8 %divide_convert_fusion = bf16[4,512,512]{1,2,0:T(8,128)(2,1)S(1)} fusion(f32[4,512,512]{1,2,0:T(8,128)} %get-tuple-element.57, f32[4,512]{1,0:T(4,128)S(1)} %get-tuple-element.56), kind=kLoop, calls=%fused_computation.2 | loop fusion | flops 2097152 | bytes 6299648 | tf_op jit(solution)/shard_map/while/body/eval_jaxpr/convert_element_type | solution.py:71
  96.4 4.4 %all-to-all-done.5 = bf16[4,128,512]{1,2,0:T(8,128)(2,1)} async-done(((bf16[4,128,512]{1,2,0:T(8,128)(2,1)}), bf16[4,128,512]{1,2,0:T(8,128)(2,1)}, u32[]{:S(2)}, u32[]{:S(2)}) %all-to-all-start.5) | async-done | bytes 524320 | tf_op jit(solution)/shard_map/all_to_all | solution.py:140
  100.8 4.3 %all-to-all-start.6 = ((bf16[4,128,512]{1,2,0:T(8,128)(2,1)}), bf16[4,128,512]{1,2,0:T(8,128)(2,1)}, u32[]{:S(2)}, u32[]{:S(2)}) async-start(bf16[4,128,512]{1,2,0:T(8,128)(2,1)} %get-tuple-element.22), calls=%async_computation.6 | async-start | bytes 1048576 | tf_op jit(solution)/shard_map/all_to_all | solution.py:141
  105.1 1.9 %fusion.54 = (bf16[512,4,128]{2,0,1:T(8,128)(2,1)S(1)}, f32[512,4,128]{2,0,1:T(8,128)}) fusion(bf16[4,512,512]{1,2,0:T(8,128)(2,1)S(1)} %divide_convert_fusion, bf16[512,4,128]{2,1,0:T(4,128)(2,1)S(1)} %reshape_squeeze.26), kind=kOutput, calls=%fused_computation.88 | convolution fusion | flops 268697600 | bytes 4194304 | tf_op jit(solution)/shard_map/while/body/eval_jaxpr/hbk,khd->bhd/dot_general | solution.py:72
  107.0 1.2 copy.48
  108.2 2.0 %reshape.438 = bf16[4,128,512]{2,1,0:T(8,128)(2,1)} reshape(bf16[512,4,128]{2,1,0:T(4,128)(2,1)} %copy.48) | data formatting | bytes 1048576 | tf_op jit(solution)/shard_map/reshape | solution.py:167
  110.2 2.0 %copy.55 = bf16[4,128,512]{2,1,0:T(8,128)(2,1)} copy(bf16[4,128,512]{1,2,0:T(8,128)(2,1)} %all-to-all-done.5) | data formatting | bytes 1048576 | tf_op jit(solution)/shard_map/all_to_all | solution.py:140
  112.3 1.9 %squeeze.14 = bf16[512,4,128]{2,1,0:T(4,128)(2,1)} reshape(bf16[4,128,512]{2,1,0:T(8,128)(2,1)} %copy.55) | data formatting | bytes 1048576 | tf_op jit(solution)/shard_map/while/body/jit(dynamic_index_in_dim)/squeeze | solution.py:164
  114.2 2.0 %reshape_squeeze.28 = bf16[512,4,128]{2,1,0:T(4,128)(2,1)} reshape(bf16[4,128,512]{2,1,0:T(8,128)(2,1)} %copy-done.8) | data formatting | bytes 1048576 | tf_op jit(solution)/shard_map/reshape;squeeze | solution.py:131
  116.2 2.9 %fusion.30 = f32[4,512,128]{2,1,0:T(8,128)} fusion(bf16[4,512,512]{1,2,0:T(8,128)(2,1)S(1)} %divide_convert_fusion, bf16[512,4,128]{2,1,0:T(4,128)(2,1)} %reshape_squeeze.28), kind=kOutput, calls=%fused_computation.41 | convolution fusion | flops 268435456 | bytes 3670016 | tf_op jit(solution)/shard_map/while/body/eval_jaxpr/hbk,khd->bhd/dot_general | solution.py:87
  119.1 3.7 %fusion.28 = f32[4,512,512]{1,2,0:T(8,128)} fusion(bf16[512,4,128]{2,1,0:T(4,128)(2,1)} %squeeze.14, bf16[512,4,128]{2,1,0:T(4,128)(2,1)S(1)} %reshape_squeeze.24), kind=kOutput, calls=%fused_computation.39 | convolution fusion | flops 268435456 | bytes 5242880 | tf_op jit(solution)/shard_map/while/body/eval_jaxpr/bhd,khd->hbk/dot_general | solution.py:80
  122.9 4.9 %all-to-all-start.3 = ((bf16[4,128,512]{2,1,0:T(8,128)(2,1)}), bf16[4,128,512]{2,1,0:T(8,128)(2,1)S(1)}, u32[]{:S(2)}, u32[]{:S(2)}) async-start(bf16[4,128,512]{2,1,0:T(8,128)(2,1)} %reshape.438), calls=%async_computation.3 | async-start | bytes 1048576 | tf_op jit(solution)/shard_map/all_to_all | solution.py:170
  127.7 2.0 %copy.60 = bf16[4,128,512]{2,1,0:T(8,128)(2,1)} copy(bf16[4,128,512]{1,2,0:T(8,128)(2,1)} %all-to-all-done.6) | data formatting | bytes 1048576 | tf_op jit(solution)/shard_map/all_to_all | solution.py:141
  129.8 2.0 %reshape_squeeze.29 = bf16[512,4,128]{2,1,0:T(4,128)(2,1)} reshape(bf16[4,128,512]{2,1,0:T(8,128)(2,1)} %copy.60) | data formatting | bytes 1048576 | tf_op jit(solution)/shard_map/reshape;squeeze | solution.py:131
  131.7 3.7 %fusion.55 = (f32[4,512]{1,0:T(4,128)S(1)}, bf16[4,512,512]{1,2,0:T(8,128)(2,1)S(1)}) fusion(f32[4,512,512]{1,2,0:T(8,128)} %fusion.28, bf16[512,4,128]{2,1,0:T(4,128)(2,1)} %reshape_squeeze.29, bf16[512,4,128]{2,1,0:T(4,128)(2,1)} %copy-done.2, bf16[4,512,512]{1,2,0:T(8,128)(2,1)S(1)} %divide_convert_fusion), kind=kOutput, calls=%fused_computation.89 | convolution fusion | flops 274724864 | bytes 9445376 | tf_op jit(solution)/shard_map/while/body/eval_jaxpr/bhd,khd->hbk/dot_general | solution.py:81
  135.4 0.9 fusion.16
  137.0 2.1 %collective-permute-start = (bf16[1,128,512]{2,1,0:T(8,128)(2,1)S(1)}, bf16[1,128,512]{2,1,0:T(8,128)(2,1)S(1)}, u32[]{:S(2)}, u32[]{:S(2)}) collective-permute-start(bf16[1,128,512]{2,1,0:T(8,128)(2,1)S(1)} %get-tuple-element.53), channel_id=1, source_target_pairs={{0,1},{1,0},{2,3},{3,2},{4,5},{5,4},{6,7},{7,6},{8,9},{9,8},{10,11... | collective-permute-start | bytes 393224 | tf_op jit(solution)/shard_map/ppermute | solution.py:25
  139.1 2.4 %collective-permute-start.1 = (bf16[1,128,512]{2,1,0:T(8,128)(2,1)S(1)}, bf16[1,128,512]{2,1,0:T(8,128)(2,1)S(1)}, u32[]{:S(2)}, u32[]{:S(2)}) collective-permute-start(bf16[1,128,512]{2,1,0:T(8,128)(2,1)S(1)} %get-tuple-element.52), channel_id=1, source_target_pairs={{0,2},{1,3},{2,0},{3,1},{4,6},{5,7},{6,4},{7,5},{8,10},{9,11},{10,... | collective-permute-start | bytes 393224 | tf_op jit(solution)/shard_map/ppermute | solution.py:25
  141.6 1.8 %collective-permute-done = bf16[1,128,512]{2,1,0:T(8,128)(2,1)S(1)} collective-permute-done((bf16[1,128,512]{2,1,0:T(8,128)(2,1)S(1)}, bf16[1,128,512]{2,1,0:T(8,128)(2,1)S(1)}, u32[]{:S(2)}, u32[]{:S(2)}) %collective-permute-start) | collective-permute-done | bytes 131104 | tf_op jit(solution)/shard_map/ppermute | solution.py:25
  143.9 6.8 %collective-permute-done.1 = bf16[1,128,512]{2,1,0:T(8,128)(2,1)S(1)} collective-permute-done((bf16[1,128,512]{2,1,0:T(8,128)(2,1)S(1)}, bf16[1,128,512]{2,1,0:T(8,128)(2,1)S(1)}, u32[]{:S(2)}, u32[]{:S(2)}) %collective-permute-start.1) | collective-permute-done | bytes 131104 | tf_op jit(solution)/shard_map/ppermute | solution.py:25
  151.1 2.2 %dynamic_update_slice.23 = bf16[4,1,128,512]{3,0,2,1:T(4,128)(2,1)S(1)} dynamic-update-slice(bf16[4,1,128,512]{3,0,2,1:T(4,128)(2,1)S(1)} %copy.66, bf16[1,1,128,512]{3,0,2,1:T(2,128)(2,1)S(1)} %copy.67, s32[]{:T(128)S(6)} %select_n.165, s32[]{:T(128)} %constant.99.clone.1, s32[]{:T(128)} %constant.99.clone.1, s32[]{:T(128)} %constant.99.clone.1) | dynamic-update-slice | bytes 262148 | tf_op jit(solution)/shard_map/dynamic_update_slice | solution.py:26
  153.3 2.2 %dynamic_update_slice.24 = bf16[4,1,128,512]{3,0,2,1:T(4,128)(2,1)S(1)} dynamic-update-slice(bf16[4,1,128,512]{3,0,2,1:T(4,128)(2,1)S(1)} %dynamic_update_slice.23, bf16[1,1,128,512]{3,0,2,1:T(2,128)(2,1)S(1)} %copy.68, s32[]{:T(128)S(6)} %select_n.166, s32[]{:T(128)} %constant.99.clone.1, s32[]{:T(128)} %constant.99.clone.1, s32[]{:T(128)} %constant.99.clone.1) | dynamic-update-slice | bytes 262148 | tf_op jit(solution)/shard_map/dynamic_update_slice | solution.py:26
  155.5 1.2 broadcast_in_dim_reshape.7
  157.0 1.0 copy.69
  (57 shorter events, 6.9 us)
Async XLA Ops:
  5.0 1.2 copy-start.5
  7.4 1.7 %copy-start = (f32[128,16,128]{0,2,1:T(8,128)}, f32[128,16,128]{0,2,1:T(8,128)S(1)}, u32[]{:S(2)}) copy-start(f32[128,16,128]{0,2,1:T(8,128)S(1)} %mul.161) | copy-start | bytes 3145732
  9.1 20.9 %all-to-all-start.1 = ((bf16[4,128,512]{1,2,0:T(8,128)(2,1)}), bf16[4,128,512]{1,2,0:T(8,128)(2,1)}, u32[]{:S(2)}, u32[]{:S(2)}) async-start(bf16[4,128,512]{1,2,0:T(8,128)(2,1)} %get-tuple-element.23), calls=%async_computation.1 | async-start | bytes 1048576 | tf_op jit(solution)/shard_map/all_to_all | solution.py:138
  19.4 1.2 copy-start.6
  19.4 1.5 copy-start.7
  21.0 1.2 copy-start.1
  23.9 27.1 %copy-start.9 = (bf16[1,128,2048]{2,1,0:T(8,128)(2,1)S(1)}, bf16[1,128,2048]{2,1,0:T(8,128)(2,1)}, u32[]{:S(2)}) copy-start(bf16[1,128,2048]{2,1,0:T(8,128)(2,1)} %param.12) | copy-start | bytes 1572868
  30.0 17.5 %all-to-all-start = ((bf16[4,128,512]{1,2,0:T(8,128)(2,1)}), bf16[4,128,512]{1,2,0:T(8,128)(2,1)S(1)}, u32[]{:S(2)}, u32[]{:S(2)}) async-start(bf16[4,128,512]{1,2,0:T(8,128)(2,1)} %get-tuple-element.25), calls=%async_computation | async-start | bytes 1048576 | tf_op jit(solution)/shard_map/all_to_all | solution.py:137
  47.5 17.5 %all-to-all-start.2 = ((bf16[4,128,512]{2,1,0:T(8,128)(2,1)}), bf16[4,128,512]{2,1,0:T(8,128)(2,1)S(1)}, u32[]{:S(2)}, u32[]{:S(2)}) async-start(bf16[4,128,512]{2,1,0:T(8,128)(2,1)} %bitcast.103), calls=%async_computation.2 | async-start | bytes 1048576 | tf_op jit(solution)/shard_map/all_to_all | solution.py:139
  65.0 17.5 %all-to-all-start.4 = ((bf16[4,128,512]{2,1,0:T(8,128)(2,1)}), bf16[4,128,512]{2,1,0:T(8,128)(2,1)S(1)}, u32[]{:S(2)}, u32[]{:S(2)}) async-start(bf16[4,128,512]{2,1,0:T(8,128)(2,1)} %bitcast.102), calls=%async_computation.4 | async-start | bytes 1048576 | tf_op jit(solution)/shard_map/all_to_all | solution.py:142
  70.2 16.4 %copy-start.2 = (bf16[512,4,128]{2,1,0:T(4,128)(2,1)}, bf16[512,4,128]{2,1,0:T(4,128)(2,1)S(1)}, u32[]{:S(2)}) copy-start(bf16[512,4,128]{2,1,0:T(4,128)(2,1)S(1)} %squeeze.13) | copy-start | bytes 1572868
  82.5 10.9 %copy-start.8 = (bf16[4,128,512]{2,1,0:T(8,128)(2,1)}, bf16[4,128,512]{2,1,0:T(8,128)(2,1)S(1)}, u32[]{:S(2)}) copy-start(bf16[4,128,512]{2,1,0:T(8,128)(2,1)S(1)} %all-to-all-done.4) | copy-start | bytes 1572868
  82.5 18.3 %all-to-all-start.5 = ((bf16[4,128,512]{1,2,0:T(8,128)(2,1)}), bf16[4,128,512]{1,2,0:T(8,128)(2,1)}, u32[]{:S(2)}, u32[]{:S(2)}) async-start(bf16[4,128,512]{1,2,0:T(8,128)(2,1)} %get-tuple-element.24), calls=%async_computation.5 | async-start | bytes 1048576 | tf_op jit(solution)/shard_map/all_to_all | solution.py:140
  100.8 22.1 %all-to-all-start.6 = ((bf16[4,128,512]{1,2,0:T(8,128)(2,1)}), bf16[4,128,512]{1,2,0:T(8,128)(2,1)}, u32[]{:S(2)}, u32[]{:S(2)}) async-start(bf16[4,128,512]{1,2,0:T(8,128)(2,1)} %get-tuple-element.22), calls=%async_computation.6 | async-start | bytes 1048576 | tf_op jit(solution)/shard_map/all_to_all | solution.py:141
  122.9 33.8 %all-to-all-start.3 = ((bf16[4,128,512]{2,1,0:T(8,128)(2,1)}), bf16[4,128,512]{2,1,0:T(8,128)(2,1)S(1)}, u32[]{:S(2)}, u32[]{:S(2)}) async-start(bf16[4,128,512]{2,1,0:T(8,128)(2,1)} %reshape.438), calls=%async_computation.3 | async-start | bytes 1048576 | tf_op jit(solution)/shard_map/all_to_all | solution.py:170
  131.7 3.7 %copy-start.3 = (f32[4,512,128]{2,1,0:T(8,128)S(1)}, f32[4,512,128]{2,1,0:T(8,128)}, u32[]{:S(2)}) copy-start(f32[4,512,128]{2,1,0:T(8,128)} %fusion.30) | copy-start | bytes 3145732
  131.7 3.7 %copy-start.4 = (f32[512,4,128]{2,0,1:T(8,128)S(1)}, f32[512,4,128]{2,0,1:T(8,128)}, u32[]{:S(2)}) copy-start(f32[512,4,128]{2,0,1:T(8,128)} %get-tuple-element.59) | copy-start | bytes 3145732
  137.0 6.4 %collective-permute-start = (bf16[1,128,512]{2,1,0:T(8,128)(2,1)S(1)}, bf16[1,128,512]{2,1,0:T(8,128)(2,1)S(1)}, u32[]{:S(2)}, u32[]{:S(2)}) collective-permute-start(bf16[1,128,512]{2,1,0:T(8,128)(2,1)S(1)} %get-tuple-element.53), channel_id=1, source_target_pairs={{0,1},{1,0},{2,3},{3,2},{4,5},{5,4},{6,7},{7,6},{8,9},{9,8},{10,11... | collective-permute-start | bytes 393224 | tf_op jit(solution)/shard_map/ppermute | solution.py:25
  139.1 11.5 %collective-permute-start.1 = (bf16[1,128,512]{2,1,0:T(8,128)(2,1)S(1)}, bf16[1,128,512]{2,1,0:T(8,128)(2,1)S(1)}, u32[]{:S(2)}, u32[]{:S(2)}) collective-permute-start(bf16[1,128,512]{2,1,0:T(8,128)(2,1)S(1)} %get-tuple-element.52), channel_id=1, source_target_pairs={{0,2},{1,3},{2,0},{3,1},{4,6},{5,7},{6,4},{7,5},{8,10},{9,11},{10,... | collective-permute-start | bytes 393224 | tf_op jit(solution)/shard_map/ppermute | solution.py:25
  141.5 9.4 %collective-permute-start.2 = (bf16[1,128,512]{2,1,0:T(8,128)(2,1)S(1)}, bf16[1,128,512]{2,1,0:T(8,128)(2,1)S(1)}, u32[]{:S(2)}, u32[]{:S(2)}) collective-permute-start(bf16[1,128,512]{2,1,0:T(8,128)(2,1)S(1)} %get-tuple-element.51), channel_id=1, source_target_pairs={{0,3},{1,2},{2,1},{3,0},{4,7},{5,6},{6,5},{7,4},{8,11},{9,10},{10,... | collective-permute-start | bytes 393224 | tf_op jit(solution)/shard_map/ppermute | solution.py:25
